TPU v7x, 32 devices: a whole 2x2x4 slice. The times are simulated.
32 devices in a mesh: les: 8 (over y, x, core), modes: 4 (over z).
Axes of the slice: x: 2, y: 2, z: 4, core: 2. Of those that a mesh axis runs over, the one named last changes fastest.
Arguments:
- pressure: bfloat16 [65536, 512], P('les', 'modes'), may hold values from -6 to 6
- targets: int32 [65536], P('les'), may hold values from 0 to 32767, as said below
- counts: int32 [8], P('les'), may hold values from 1 to 8192, as said below
- pseudo_inverse: bfloat16 [2, 1536, 16384], P(None, None, ('les', 'modes')), may hold values from -0.046875 to 0.046875
Outputs:
- harmonics: float32 [2, 2, 8, 1536], P(None, None, None, ('les', 'modes'))
Inputs may be any that keep to these rules, and one draw needn't show every extreme that they name: `counts`: some partition holds exactly 8192 live faces; all partitions together hold 32768. `targets`: the live slots (slot f of partition i with f < counts[i]) name every station point exactly once. Point p of a station lies in the point rows of les index p // (512 * 4); at most 1024 live faces of one partition lie in the point rows of one les index, and some partition reaches that bound. Slots that are not live hold arbitrary indices in the range.
All inputs are finite; a program needn't handle non-finite values.
Results may differ from a plain program's by a relative error of at most 0.0003.
Values may be sent and summed in bfloat16 or wider, within the bound.
A program may use at most 64 MiB of HBM per device.

v0:
```python
import math
import jax
import jax.numpy as jnp
from jax import lax
from jax.sharding import PartitionSpec as P

TIME = 512
HARM = 8


def fourier_rows():
    sample_ids = jnp.arange(TIME, dtype=jnp.int32)
    orders = jnp.arange(1, HARM + 1, dtype=jnp.int32)
    phase_ids = orders[:, None] * sample_ids[None, :] % TIME
    angles = phase_ids.astype(jnp.float32) * (2.0 * math.pi / TIME)
    scale_factor = math.sqrt(2.0 / TIME)
    return jnp.stack([jnp.cos(angles), -jnp.sin(angles)]) * scale_factor


def rank_by_owner(dest_les, is_live, les_count):
    face_slots = dest_les.shape[0]
    span_width = math.gcd(face_slots, 128)
    owner_ids = jnp.arange(les_count, dtype=jnp.int32)
    matches = ((dest_les[None, :] == owner_ids[:, None]) & is_live[None, :]).astype(jnp.float32)
    matches = matches.reshape(les_count, face_slots // span_width, span_width)
    position = jnp.arange(span_width, dtype=jnp.int32)
    upper = (position[:, None] <= position[None, :]).astype(jnp.float32)
    within = jnp.einsum("nbj,jw->nbw", matches, upper, precision=lax.Precision.HIGHEST)
    block_sums = jnp.sum(matches, axis=2)
    before = jnp.cumsum(block_sums, axis=1) - block_sums
    running = within + before[:, :, None]
    ranked = jnp.sum(running * matches, axis=0).reshape(face_slots) - 1.0
    return ranked.astype(jnp.int32)


def local(pressure, targets, counts, pseudo_inverse):
    les_count = lax.axis_size("les")
    mode_count = lax.axis_size("modes")
    block_len = pressure.shape[1]
    face_slots = targets.shape[0]
    stations = pseudo_inverse.shape[0]
    mode_total = pseudo_inverse.shape[1]
    point_dev = pseudo_inverse.shape[2]
    rows_les = point_dev * mode_count
    points_all = rows_les * les_count
    send_cap = face_slots // les_count
    send_total = les_count * send_cap
    slot_ids = jnp.arange(face_slots, dtype=jnp.int32)
    is_live = slot_ids < counts[0]
    station_of = targets // points_all
    point_of = targets % points_all
    dest_les = point_of // rows_les
    local_row = station_of * rows_les + point_of % rows_les
    face_rank = rank_by_owner(dest_les, is_live, les_count)
    send_pos = jnp.where(is_live, dest_les * send_cap + face_rank, send_total)
    source_face = jnp.full((send_total,), -1, jnp.int32).at[send_pos].set(slot_ids, mode="drop")
    slot_used = source_face >= 0
    source_safe = jnp.maximum(source_face, 0)
    row_tags = jnp.where(slot_used, jnp.take(local_row, source_safe, axis=0), -1).reshape(
        1, send_total
    )
    tags_in = lax.all_to_all(row_tags, "les", split_axis=1, concat_axis=1, tiled=True)
    arrival = jnp.where(tags_in[0] >= 0, tags_in[0], stations * rows_les)
    arrival_ids = jnp.arange(send_total, dtype=jnp.int32)
    arrived_from = (
        jnp.zeros((stations * rows_les,), jnp.int32).at[arrival].set(arrival_ids, mode="drop")
    )
    fourier = fourier_rows()
    block_start = lax.axis_index("modes") * block_len
    block_rows = lax.dynamic_slice_in_dim(fourier, block_start, block_len, 2)
    block_rows = block_rows.reshape(2 * HARM, block_len)
    spectra = lax.dot_general(
        pressure.astype(jnp.float32),
        block_rows,
        (((1,), (1,)), ((), ())),
        precision=lax.Precision.HIGHEST,
    )
    picked = jnp.take(spectra, source_safe, axis=0)
    outgoing = jnp.where(slot_used[:, None], picked, jnp.zeros_like(picked))
    incoming = lax.all_to_all(outgoing, "les", split_axis=0, concat_axis=0, tiled=True)
    gathered = jnp.take(incoming, arrived_from, axis=0)
    gathered = gathered.reshape(stations, rows_les, 2 * HARM)
    summed = lax.psum_scatter(gathered, "modes", scatter_dimension=1, tiled=True)
    partial_value = []
    for station_index in range(stations):
        weights = pseudo_inverse[station_index].astype(jnp.float32)
        projected = lax.dot_general(
            summed[station_index],
            weights,
            (((0,), (1,)), ((), ())),
            precision=lax.Precision.HIGHEST,
        )
        partial_value.append(projected.reshape(2, HARM, mode_total))
    shares = jnp.stack(partial_value)
    return lax.psum_scatter(shares, ("les", "modes"), scatter_dimension=3, tiled=True)


def solution(mesh):
    placed = (P("les", "modes"), P("les"), P("les"), P(None, None, ("les", "modes")))
    return jax.shard_map(
        local,
        mesh=mesh,
        in_specs=placed,
        out_specs=P(None, None, None, ("les", "modes")),
        check_vma=False,
    )
```

profile of v0, /device:TPU:0, one launch (start us, length us, event | category | flops | bytes accessed | tf_op | source)
XLA Modules:
  0.0 323.5 jit_solution(5124301517689672651)
XLA Ops:
  7.4 0.8 fusion.13
  8.8 0.8 compare_select_fusion.2
  9.6 30.5 %scatter_custom_fusion = s32[8192]{0:T(1024)S(1)} fusion(s32[8192]{0:T(1024)S(1)} %compare_select_fusion.2, s32[8192]{0:T(1024)S(1)} %iota.64, s32[]{:T(128)} %constant.117.clone.1), kind=kCustom, calls=%fused_computation.68 | custom fusion | bytes 32772 | tf_op jit(solution)/shard_map/scatter | solution.py:56
  40.1 45.5 %gather_fusion = s32[8192]{0:T(1024)S(1)} fusion(s32[8192]{0:T(1024)S(1)} %get-tuple-element.8, s32[8192]{0:T(1024)S(1)} %maximum_clamp_fusion), kind=kCustom, calls=%fused_computation | custom fusion | bytes 98304 | tf_op jit(solution)/shard_map/jit(_take)/gather | solution.py:59
  86.3 5.2 %all-to-all-start = ((s32[1,8,1024]{2,0,1:T(1,128)}), s32[1,8,1024]{2,0,1:T(1,128)S(1)}, u32[]{:S(2)}, u32[]{:S(2)}) async-start(s32[1,8,1024]{2,0,1:T(1,128)} %bitcast.4), calls=%async_computation | async-start | bytes 65536 | tf_op jit(solution)/shard_map/all_to_all | solution.py:62
  91.7 1.7 convolution_bitcast_fusion
  93.4 2.6 copy.9
  96.0 29.9 %gather_fusion.1 = f32[8192,16]{1,0:T(8,128)} fusion(f32[8192,16]{1,0:T(8,128)} %copy.9, s32[8192]{0:T(1024)S(1)} %maximum_clamp_fusion), kind=kCustom, calls=%fused_computation.1 | custom fusion | bytes 1081344 | tf_op jit(solution)/shard_map/jit(_take)/gather | solution.py:78
  125.9 2.8 copy.10
  128.7 0.9 select_select_fusion
  129.6 4.2 %all-to-all-start.1 = ((f32[8,1024,16]{1,2,0:T(8,128)}), f32[8,1024,16]{1,2,0:T(8,128)S(1)}, u32[]{:S(2)}, u32[]{:S(2)}) async-start(f32[8,1024,16]{1,2,0:T(8,128)} %select_select_fusion), calls=%async_computation.1 | async-start | bytes 1048576 | tf_op jit(solution)/shard_map/all_to_all | solution.py:80
  133.9 30.5 %scatter_custom_fusion.1 = s32[4096]{0:T(1024)S(1)} fusion(s32[8192]{0:T(1024)S(1)} %bitcast.62, s32[8192]{0:T(1024)S(1)} %iota.65, s32[]{:T(128)} %constant.116.clone.1), kind=kCustom, calls=%fused_computation.77 | custom fusion | bytes 16388 | tf_op jit(solution)/shard_map/scatter | solution.py:66
  164.4 2.6 copy.11
  167.0 16.3 %gather_fusion.2 = f32[4096,16]{1,0:T(8,128)} fusion(f32[8192,16]{1,0:T(8,128)} %bitcast.56, s32[4096]{0:T(1024)S(1)} %fusion.27), kind=kCustom, calls=%fused_computation.2 | custom fusion | bytes 540672 | tf_op jit(solution)/shard_map/jit(_take)/gather | solution.py:81
  183.3 2.2 copy.12
  185.4 0.7 broadcast_select_fusion
  186.2 21.4 %reduce-scatter.5.cloned.1.call-done = f32[2,512,16]{1,2,0:T(8,128)} async-done(((f32[2,2048,16]{1,2,0:T(8,128)}), f32[2,512,16]{1,2,0:T(8,128)}) %reduce-scatter.5.cloned.1.call-update) | async-done | bytes 65552 | tf_op jit(solution)/shard_map/reduce_scatter | solution.py:83
  207.7 2.7 convolution_bitcast_fusion.1
  210.4 2.8 convolution_bitcast_fusion.2
  213.2 3.3 %copy.13 = f32[2,2,8,1536]{2,1,0,3:T(2,128)} copy(f32[2,2,8,1536]{3,2,1,0:T(8,128)S(1)} %pad_maximum_fusion) | data formatting | bytes 393216
  216.5 4.7 %reshape.276 = f32[1536,32]{1,0:T(8,128)} reshape(f32[1536,2,2,8]{3,2,1,0:T(2,128)} %bitcast.58) | data formatting | bytes 393216
  221.2 93.9 %reduce-scatter.7.cloned.1.call-done = f32[48,32]{1,0:T(8,128)} async-done(((f32[1536,32]{1,0:T(8,128)}), f32[48,32]{1,0:T(8,128)}) %reduce-scatter.7.cloned.1.call-update) | async-done | bytes 6160
  315.1 0.9 reshape.277
  315.9 0.7 copy.14
  (26 shorter events, 1.6 us)
Async XLA Ops:
  6.5 85.1 %copy-start = (bf16[8192,128]{1,0:T(8,128)(2,1)S(1)}, bf16[8192,128]{1,0:T(8,128)(2,1)}, u32[]{:S(2)}) copy-start(bf16[8192,128]{1,0:T(8,128)(2,1)} %param.4) | copy-start | bytes 6291460
  86.3 43.3 %all-to-all-start = ((s32[1,8,1024]{2,0,1:T(1,128)}), s32[1,8,1024]{2,0,1:T(1,128)S(1)}, u32[]{:S(2)}, u32[]{:S(2)}) async-start(s32[1,8,1024]{2,0,1:T(1,128)} %bitcast.4), calls=%async_computation | async-start | bytes 65536 | tf_op jit(solution)/shard_map/all_to_all | solution.py:62
  129.6 34.8 %all-to-all-start.1 = ((f32[8,1024,16]{1,2,0:T(8,128)}), f32[8,1024,16]{1,2,0:T(8,128)S(1)}, u32[]{:S(2)}, u32[]{:S(2)}) async-start(f32[8,1024,16]{1,2,0:T(8,128)} %select_select_fusion), calls=%async_computation.1 | async-start | bytes 1048576 | tf_op jit(solution)/shard_map/all_to_all | solution.py:80
  133.8 73.9 %reduce-scatter.5.cloned.1.call-start = ((), (), s32[]{:S(2)}) async-start(), calls=%async_computation.4 | async-start | bytes 327680 | tf_op jit(solution)/shard_map/reduce_scatter | solution.py:83
  186.2 128.9 %reduce-scatter.7.cloned.1.call-start = ((), (), s32[]{:S(2)}) async-start(), calls=%async_computation.5 | async-start | bytes 811008
Sparse Core Ops, SparseCore 0:
  186.3 21.3 reduce-scatter.4
  221.3 93.6 reduce-scatter.6
where the time goes:
time: 324 us; the launch traced here: 323 us
  local copies, waits for them, and re-layouts  172 us (53%)
  waiting for transfers between devices  115 us (35%)
  between operations  14.4 us (4%)
  starting transfers between devices  9.44 us (3%)
  matrix products  7.45 us (2%)
  other arithmetic  4.52 us (1%)
    unnamed x3, waiting for transfers between devices  93.9 us
    gather x1, local copies, waits for them, and re-layouts, local(): jnp.take(local_row, source_safe, axis=0)  45.5 us
    gather x2, local copies, waits for them, and re-layouts, local(): picked = jnp.take(spectra, source_safe, axis=0)  32.7 us
    scatter x1, local copies, waits for them, and re-layouts, local(): jnp.full((send_total,), -1, jnp.int32).at[send_pos]  30.5 us
    scatter x1, local copies, waits for them, and re-layouts, local(): jnp.zeros((stations * rows_les,), jnp.int32).at[arrival]  30.5 us
    reduce_scatter x1, waiting for transfers between devices, local(): lax.psum_scatter(gathered, 'modes', scatter_dimension=1, tiled=True)  21.4 us
    gather x2, local copies, waits for them, and re-layouts, local(): gathered = jnp.take(incoming, arrived_from, axis=0)  18.4 us
    unnamed x6, local copies, waits for them, and re-layouts  9.54 us
  transfers between devices with their start and end apart: 4, of which 2 were waited for; matrix products, arithmetic and copies ran while one was open for 21% of the time, Pallas kernels for 0%

commit v1 on v0

--- a/solution.py
+++ b/solution.py
@@ -6,6 +6,28 @@
 
 TIME = 512
 HARM = 8
+
+
+def in_blocks(array, dim, peers):
+    before, after = (array.shape[:dim], array.shape[dim + 1 :])
+    return jnp.moveaxis(array.reshape(*before, peers, -1, *after), dim, 0)
+
+
+def in_order(blocks, dim):
+    lengths = list(blocks.shape[1:])
+    lengths[dim] *= blocks.shape[0]
+    return jnp.moveaxis(blocks, 0, dim).reshape(lengths)
+
+
+def pairwise_exchange(array, axis, split_dim, concat_dim):
+    size, index = (lax.axis_size(axis), lax.axis_index(axis))
+    tiles = in_blocks(array, split_dim, size)
+    outs = [tiles[index]]
+    for step in range(1, size):
+        sent = tiles[index ^ step]
+        outs.append(lax.ppermute(sent, axis, [(i, i ^ step) for i in range(size)]))
+    tiles = jnp.stack(outs)[index ^ jnp.arange(size)]
+    return in_order(tiles, concat_dim)
 
 
 def fourier_rows():
@@ -77,7 +99,7 @@
     )
     picked = jnp.take(spectra, source_safe, axis=0)
     outgoing = jnp.where(slot_used[:, None], picked, jnp.zeros_like(picked))
-    incoming = lax.all_to_all(outgoing, "les", split_axis=0, concat_axis=0, tiled=True)
+    incoming = pairwise_exchange(outgoing, "les", 0, 0)
     gathered = jnp.take(incoming, arrived_from, axis=0)
     gathered = gathered.reshape(stations, rows_les, 2 * HARM)
     summed = lax.psum_scatter(gathered, "modes", scatter_dimension=1, tiled=True)

time: 324 us -> 333 us (1.028)
  waiting for transfers between devices: 115 us -> 121 us
    ppermute x0 -> x7, starting transfers between devices: none -> 7.44 us  [pairwise_exchange(): outs.append(lax.ppermute(sent, axis, [(i, i ^ step) for i in range(size)]))]
    ppermute x0 -> x7, waiting for transfers between devices: none -> 6.04 us  [pairwise_exchange(): outs.append(lax.ppermute(sent, axis, [(i, i ^ step) for i in range(size)]))]
    all_to_all x1 -> x0, starting transfers between devices: 4.2 us -> none  [local(): lax.all_to_all(outgoing, 'les', split_axis=0, concat_axis=0, tiled=True)]
    unnamed x6 -> x12, local copies, waits for them, and re-layouts: 9.54 us -> 9.53 us
  transfers between devices with their start and end apart: 4 -> 10, of which waited for: 2 -> 4; matrix products, arithmetic and copies ran while one was open for 21% -> 20% of each run, Pallas kernels for 0% -> 0%
where the time goes in v1:
time: 333 us; the launch traced here: 332 us
  local copies, waits for them, and re-layouts  173 us (52%)
  waiting for transfers between devices  121 us (36%)
  between operations  14.5 us (4%)
  starting transfers between devices  12.7 us (4%)
  matrix products  7.45 us (2%)
  other arithmetic  3.74 us (1%)
    unnamed x3, waiting for transfers between devices  93.9 us
    gather x1, local copies, waits for them, and re-layouts, local(): jnp.take(local_row, source_safe, axis=0)  45.5 us
    gather x2, local copies, waits for them, and re-layouts, local(): picked = jnp.take(spectra, source_safe, axis=0)  32.7 us
    scatter x1, local copies, waits for them, and re-layouts, local(): jnp.full((send_total,), -1, jnp.int32).at[send_pos]  30.5 us
    scatter x1, local copies, waits for them, and re-layouts, local(): jnp.zeros((stations * rows_les,), jnp.int32).at[arrival]  30.5 us
    reduce_scatter x1, waiting for transfers between devices, local(): lax.psum_scatter(gathered, 'modes', scatter_dimension=1, tiled=True)  21.1 us
    gather x2, local copies, waits for them, and re-layouts, local(): gathered = jnp.take(incoming, arrived_from, axis=0)  18.4 us
    unnamed x12, local copies, waits for them, and re-layouts  9.53 us
  transfers between devices with their start and end apart: 10, of which 4 were waited for; matrix products, arithmetic and copies ran while one was open for 20% of the time, Pallas kernels for 0%

profile of v1, /device:TPU:0, one launch (start us, length us, event | category | flops | bytes accessed | tf_op | source)
XLA Modules:
  0.0 332.4 jit_solution(5239452944303648285)
XLA Ops:
  7.4 0.8 fusion.13
  9.6 30.5 %scatter_custom_fusion = s32[8192]{0:T(1024)S(1)} fusion(s32[8192]{0:T(1024)S(1)} %compare_select_fusion.2, s32[8192]{0:T(1024)S(1)} %iota.68, s32[]{:T(128)} %constant.130.clone.1), kind=kCustom, calls=%fused_computation.84 | custom fusion | bytes 32772 | tf_op jit(solution)/shard_map/scatter | solution.py:78
  40.1 45.5 %gather_fusion = s32[8192]{0:T(1024)S(1)} fusion(s32[8192]{0:T(1024)S(1)} %get-tuple-element.16, s32[8192]{0:T(1024)S(1)} %maximum_clamp_fusion), kind=kCustom, calls=%fused_computation | custom fusion | bytes 98304 | tf_op jit(solution)/shard_map/jit(_take)/gather | solution.py:81
  86.3 5.2 %all-to-all-start = ((s32[1,8,1024]{2,0,1:T(1,128)}), s32[1,8,1024]{2,0,1:T(1,128)S(1)}, u32[]{:S(2)}, u32[]{:S(2)}) async-start(s32[1,8,1024]{2,0,1:T(1,128)} %bitcast.4), calls=%async_computation | async-start | bytes 65536 | tf_op jit(solution)/shard_map/all_to_all | solution.py:84
  91.8 1.7 convolution_bitcast_fusion
  93.5 2.6 copy.9
  96.1 29.9 %gather_fusion.1 = f32[8192,16]{1,0:T(8,128)} fusion(f32[8192,16]{1,0:T(8,128)} %copy.9, s32[8192]{0:T(1024)S(1)} %maximum_clamp_fusion), kind=kCustom, calls=%fused_computation.1 | custom fusion | bytes 1081344 | tf_op jit(solution)/shard_map/jit(_take)/gather | solution.py:100
  126.0 2.8 copy.10
  129.0 2.7 collective-permute-start.6
  132.0 1.3 collective-permute-start.4
  134.0 30.5 %scatter_custom_fusion.1 = s32[4096]{0:T(1024)S(1)} fusion(s32[8192]{0:T(1024)S(1)} %bitcast.92, s32[8192]{0:T(1024)S(1)} %iota.69, s32[]{:T(128)} %constant.129.clone.1), kind=kCustom, calls=%fused_computation.93 | custom fusion | bytes 16388 | tf_op jit(solution)/shard_map/scatter | solution.py:88
  164.5 1.7 collective-permute-start.1
  166.3 2.7 collective-permute-done.1
  169.8 3.4 %collective-permute-done.2 = f32[1024,16]{0,1:T(8,128)S(1)} collective-permute-done((f32[1024,16]{0,1:T(8,128)S(1)}, f32[1024,16]{0,1:T(8,128)S(1)}, u32[]{:S(2)}, u32[]{:S(2)}) %collective-permute-start.2) | collective-permute-done | bytes 65568 | tf_op jit(solution)/shard_map/ppermute | solution.py:28
  173.8 2.6 copy.11
  176.4 16.3 %gather_fusion.3 = f32[4096,16]{1,0:T(8,128)} fusion(f32[8192,16]{1,0:T(8,128)} %bitcast.86, s32[4096]{0:T(1024)S(1)} %fusion.27), kind=kCustom, calls=%fused_computation.3 | custom fusion | bytes 540672 | tf_op jit(solution)/shard_map/jit(_take)/gather | solution.py:103
  192.7 2.2 copy.12
  195.7 21.1 %reduce-scatter.5.cloned.1.call-done = f32[2,512,16]{1,2,0:T(8,128)} async-done(((f32[2,2048,16]{1,2,0:T(8,128)}), f32[2,512,16]{1,2,0:T(8,128)}) %reduce-scatter.5.cloned.1.call-update) | async-done | bytes 65552 | tf_op jit(solution)/shard_map/reduce_scatter | solution.py:105
  216.7 2.7 convolution_bitcast_fusion.1
  219.5 2.8 convolution_bitcast_fusion.2
  222.3 3.3 copy.13
  225.5 4.7 %reshape.303 = f32[1536,32]{1,0:T(8,128)} reshape(f32[1536,2,2,8]{3,2,1,0:T(2,128)} %bitcast.88) | data formatting | bytes 393216
  230.2 93.8 %reduce-scatter.7.cloned.1.call-done = f32[48,32]{1,0:T(8,128)} async-done(((f32[1536,32]{1,0:T(8,128)}), f32[48,32]{1,0:T(8,128)}) %reduce-scatter.7.cloned.1.call-update) | async-done | bytes 6160
  324.0 0.9 reshape.304
  (49 shorter events, 6.4 us)
Async XLA Ops:
  6.5 85.2 %copy-start = (bf16[8192,128]{1,0:T(8,128)(2,1)S(1)}, bf16[8192,128]{1,0:T(8,128)(2,1)}, u32[]{:S(2)}) copy-start(bf16[8192,128]{1,0:T(8,128)(2,1)} %param.4) | copy-start | bytes 6291460
  86.3 47.6 %all-to-all-start = ((s32[1,8,1024]{2,0,1:T(1,128)}), s32[1,8,1024]{2,0,1:T(1,128)S(1)}, u32[]{:S(2)}, u32[]{:S(2)}) async-start(s32[1,8,1024]{2,0,1:T(1,128)} %bitcast.4), calls=%async_computation | async-start | bytes 65536 | tf_op jit(solution)/shard_map/all_to_all | solution.py:84
  91.4 125.3 %reduce-scatter.5.cloned.1.call-start = ((), (), s32[]{:S(2)}) async-start(), calls=%async_computation.3 | async-start | bytes 327680 | tf_op jit(solution)/shard_map/reduce_scatter | solution.py:105
  129.0 44.2 %collective-permute-start.6 = (f32[1024,16]{0,1:T(8,128)S(1)}, f32[1024,16]{0,1:T(8,128)S(1)}, u32[]{:S(2)}, u32[]{:S(2)}) collective-permute-start(f32[1024,16]{0,1:T(8,128)S(1)} %get-tuple-element.8), channel_id=1, source_target_pairs={{0,28},{4,24},{8,20},{12,16},{16,12},{20,8},{24,4},{28,0},{1,29},{... | collective-permute-start | bytes 196616 | tf_op jit(solution)/shard_map/ppermute | solution.py:28
  131.7 41.5 %collective-permute-start.5 = (f32[1024,16]{0,1:T(8,128)S(1)}, f32[1024,16]{0,1:T(8,128)S(1)}, u32[]{:S(2)}, u32[]{:S(2)}) collective-permute-start(f32[1024,16]{0,1:T(8,128)S(1)} %get-tuple-element.9), channel_id=1, source_target_pairs={{0,24},{4,28},{8,16},{12,20},{16,8},{20,12},{24,0},{28,4},{1,25},{... | collective-permute-start | bytes 196616 | tf_op jit(solution)/shard_map/ppermute | solution.py:28
  132.0 41.1 %collective-permute-start.4 = (f32[1024,16]{0,1:T(8,128)S(1)}, f32[1024,16]{0,1:T(8,128)S(1)}, u32[]{:S(2)}, u32[]{:S(2)}) collective-permute-start(f32[1024,16]{0,1:T(8,128)S(1)} %get-tuple-element.10), channel_id=1, source_target_pairs={{0,20},{4,16},{8,28},{12,24},{16,4},{20,0},{24,12},{28,8},{1,21},{... | collective-permute-start | bytes 196616 | tf_op jit(solution)/shard_map/ppermute | solution.py:28
  133.4 39.7 %collective-permute-start.3 = (f32[1024,16]{0,1:T(8,128)S(1)}, f32[1024,16]{0,1:T(8,128)S(1)}, u32[]{:S(2)}, u32[]{:S(2)}) collective-permute-start(f32[1024,16]{0,1:T(8,128)S(1)} %get-tuple-element.11), channel_id=1, source_target_pairs={{0,16},{4,20},{8,24},{12,28},{16,0},{20,4},{24,8},{28,12},{1,17},{... | collective-permute-start | bytes 196616 | tf_op jit(solution)/shard_map/ppermute | solution.py:28
  133.7 30.8 %collective-permute-start = (f32[1024,16]{0,1:T(8,128)S(1)}, f32[1024,16]{0,1:T(8,128)S(1)}, u32[]{:S(2)}, u32[]{:S(2)}) collective-permute-start(f32[1024,16]{0,1:T(8,128)S(1)} %get-tuple-element.14), channel_id=1, source_target_pairs={{0,4},{4,0},{8,12},{12,8},{16,20},{20,16},{24,28},{28,24},{1,5},{5... | collective-permute-start | bytes 196616 | tf_op jit(solution)/shard_map/ppermute | solution.py:28
  164.5 4.4 %collective-permute-start.1 = (f32[1024,16]{0,1:T(8,128)S(1)}, f32[1024,16]{0,1:T(8,128)S(1)}, u32[]{:S(2)}, u32[]{:S(2)}) collective-permute-start(f32[1024,16]{0,1:T(8,128)S(1)} %get-tuple-element.13), channel_id=1, source_target_pairs={{0,8},{4,12},{8,0},{12,4},{16,24},{20,28},{24,16},{28,20},{1,9},{5... | collective-permute-start | bytes 196616 | tf_op jit(solution)/shard_map/ppermute | solution.py:28
  168.9 4.2 %collective-permute-start.2 = (f32[1024,16]{0,1:T(8,128)S(1)}, f32[1024,16]{0,1:T(8,128)S(1)}, u32[]{:S(2)}, u32[]{:S(2)}) collective-permute-start(f32[1024,16]{0,1:T(8,128)S(1)} %get-tuple-element.12), channel_id=1, source_target_pairs={{0,12},{4,8},{8,4},{12,0},{16,28},{20,24},{24,20},{28,16},{1,13},{... | collective-permute-start | bytes 196616 | tf_op jit(solution)/shard_map/ppermute | solution.py:28
  195.6 128.4 %reduce-scatter.7.cloned.1.call-start = ((), (), s32[]{:S(2)}) async-start(), calls=%async_computation.4 | async-start | bytes 811008
Sparse Core Ops, SparseCore 0:
  195.7 20.9 reduce-scatter.4
  230.3 93.6 reduce-scatter.6
